TPU v7x, 256 devices: a whole 4x4x8 slice. The times are simulated.
256 devices in a mesh: seq: 64 (over y, z, core), pool: 4 (over x).
Axes of the slice: x: 4, y: 4, z: 8, core: 2. Of those that a mesh axis runs over, the one named last changes fastest.
Arguments:
- query_rows: bfloat16 [32768, 4096], P('seq', 'pool'), may hold values from -6 to 6
- key_rows: bfloat16 [32768, 4096], P('seq', 'pool'), may hold values from -6 to 6
- value_rows: bfloat16 [32768, 4096], P('seq', 'pool'), may hold values from -6 to 6
- log_decay: float32 [32, 32768], P('pool', 'seq'), may hold values from -0.7 to 0
- residual: bfloat16 [32768, 4096], P(('seq', 'pool')), may hold values from -6 to 6
- out_weight: bfloat16 [4096, 4096], P('pool', 'seq'), may hold values from -0.09375 to 0.09375
- norm_gain: float32 [4096], replicated, may hold values from 0.5 to 1.5
- kv_weight: bfloat16 [4096, 1024], P('seq'), may hold values from -0.09375 to 0.09375
- block_table: int32 [256, 2], P(('seq', 'pool')), may hold values from 0 to 3, as said below
Outputs:
- page_cache: bfloat16 [64, 4, 2, 128, 1024], P('seq', 'pool')
Inputs may be any that keep to these rules, and one draw needn't show every extreme that they name: `block_table`: column 0 is a page's pool device, column 1 its slot there. The pages of one index of seq go to pool devices of that same index, no two to the same device and slot; one pool device receives exactly 2 of them, each other at most 2, and all 1 pages of some device go to that one.
All inputs are finite; a program needn't handle non-finite values.
Results may differ from a plain program's by a relative error of at most 0.0056.
Values may be sent and summed in bfloat16 or wider, within the bound.
A program may use at most 128 MiB of HBM per device.

v0:
```python
import jax
import jax.numpy as jnp
from jax import lax
from jax.sharding import PartitionSpec as P

HD = 128
PAGE = 128
BLK = 512


def entering(part, axis, combine, identity):
    place = lax.axis_index(axis)
    gathered = jax.tree.map(lambda a: lax.all_gather(a, axis), part)
    state = jax.tree.map(lambda a, e: jnp.zeros_like(a) + jnp.asarray(e, a.dtype), part, identity)

    def one(hop, state):
        return combine(
            state, jax.tree.map(lambda a: lax.dynamic_index_in_dim(a, hop, 0, False), gathered)
        )

    return lax.fori_loop(0, place, one, state)


def head_major(matrix, head_count):
    return matrix.reshape(BLK, head_count, HD).transpose(1, 0, 2)


def combine_states(earlier, later):
    return (earlier[0] + later[0], jnp.exp(later[0])[:, None, None] * earlier[1] + later[1])


def on_device(
    query_rows,
    key_rows,
    value_rows,
    log_decay,
    residual,
    out_weight,
    norm_gain,
    kv_weight,
    block_table,
):
    head_count = query_rows.shape[1] // HD
    lower_mask = jnp.tril(jnp.ones((BLK, BLK), dtype=bool))
    query_blk = head_major(query_rows, head_count)
    key_blk = head_major(key_rows, head_count)
    value_blk = head_major(value_rows, head_count)
    cumulative = jnp.cumsum(log_decay, axis=1)
    block_total = cumulative[:, -1]
    log_gap = jnp.where(lower_mask[None], cumulative[:, :, None] - cumulative[:, None, :], 0.0)
    products = jnp.einsum("hid,hjd->hij", query_blk, key_blk, preferred_element_type=jnp.float32)
    scores = jnp.where(lower_mask[None], products * jnp.exp(log_gap), 0.0).astype(jnp.bfloat16)
    inner = jnp.einsum("hij,hjd->hid", scores, value_blk, preferred_element_type=jnp.float32)
    weighted = (
        key_blk.astype(jnp.float32) * jnp.exp(block_total[:, None] - cumulative)[:, :, None]
    ).astype(jnp.bfloat16)
    update = jnp.einsum("hjd,hje->hde", weighted, value_blk, preferred_element_type=jnp.float32)
    query_list = [query_blk]
    inner_list = [inner]
    update_list = [update]
    cumul_list = [cumulative]
    total_list = [block_total]
    state_sum = jnp.zeros((head_count, HD, HD), jnp.float32)
    block_index = 0
    state_sum = (
        jnp.exp(total_list[block_index])[:, None, None] * state_sum + update_list[block_index]
    )
    log_sum = total_list[block_index]
    incoming = entering(
        (log_sum, state_sum),
        "seq",
        combine_states,
        (jnp.zeros_like(log_sum), jnp.zeros_like(state_sum)),
    )
    carried = incoming[1]
    block_index = 0
    outer = (
        jnp.einsum(
            "hid,hde->hie",
            query_list[block_index].astype(jnp.float32),
            carried,
            precision=lax.Precision.HIGHEST,
        )
        * jnp.exp(cumul_list[block_index])[:, :, None]
    )
    retained = inner_list[block_index] + outer
    scaled = retained * lax.rsqrt(jnp.mean(retained * retained, axis=-1, keepdims=True) + 1e-05)
    mixed_list = scaled.transpose(1, 0, 2).reshape(BLK, head_count * HD).astype(jnp.bfloat16)
    partial_value = jnp.dot(
        mixed_list,
        lax.all_gather(out_weight, "seq", axis=1, tiled=True),
        preferred_element_type=jnp.float32,
    )
    summed = lax.psum_scatter(partial_value, "pool", scatter_dimension=0, tiled=True)
    hidden = residual.astype(jnp.float32) + summed
    normed = (
        hidden * lax.rsqrt(jnp.mean(hidden * hidden, axis=-1, keepdims=True) + 1e-05) * norm_gain
    ).astype(jnp.bfloat16)
    pool_count = lax.axis_size("pool")
    pages_here = block_table.shape[0]
    slot_count = 2 * pages_here
    cache_width = kv_weight.shape[1]
    owner_ids = jnp.arange(pool_count, dtype=jnp.int32)
    slot_ids = jnp.arange(slot_count, dtype=jnp.int32)
    owner_match = block_table[:, 0][:, None] == owner_ids[None, :]
    slot_match = block_table[:, 1][:, None] == slot_ids[None, :]
    placed = jnp.logical_and(owner_match[:, :, None], slot_match[:, None, :]).astype(jnp.bfloat16)
    cache_rows = jnp.dot(
        normed,
        lax.all_gather(kv_weight, "seq", axis=0, tiled=True),
        preferred_element_type=jnp.float32,
    ).astype(jnp.bfloat16)
    own_pages = cache_rows.reshape(pages_here, PAGE, cache_width)
    outgoing = jnp.where(
        owner_match.T[:, :, None, None], own_pages[None], jnp.zeros((), jnp.bfloat16)
    )
    slot_tags = placed.transpose(1, 0, 2)
    arrived, arrived_tags = (
        lax.all_to_all(outgoing, "pool", split_axis=0, concat_axis=0, tiled=True),
        lax.all_to_all(slot_tags, "pool", split_axis=0, concat_axis=0, tiled=True),
    )
    page_cache = jnp.einsum(
        "ips,ipqc->sqc", arrived_tags, arrived, preferred_element_type=jnp.float32
    ).astype(jnp.bfloat16)
    return page_cache.reshape(1, 1, slot_count, PAGE, cache_width)


def solution(mesh):
    placed = (
        P("seq", "pool"),
        P("seq", "pool"),
        P("seq", "pool"),
        P("pool", "seq"),
        P(("seq", "pool"), None),
        P("pool", "seq"),
        P(),
        P("seq", None),
        P(("seq", "pool"), None),
    )
    return jax.shard_map(
        on_device,
        mesh=mesh,
        in_specs=placed,
        out_specs=P("seq", "pool", None, None, None),
        check_vma=False,
    )
```

profile of v0, /device:TPU:1, one launch (start us, length us, event | category | flops | bytes accessed | tf_op | source)
XLA Modules:
  0.0 455.7 jit_solution(11323797303742219468)
XLA Ops:
  6.5 2.4 reduce-window.6
  8.9 0.2 slice_reduce_fusion
  9.1 0.1 exponential_bitcast_fusion.1
  9.2 0.2 slice_reduce_fusion.1
  9.4 0.1 fusion.23
  9.5 1.5 copy.46
  11.0 0.0 copy-start.9
  11.0 1.3 convolution_add_fusion
  12.3 0.0 all-gather.10.cloned.1.call-update
  12.3 0.0 all-gather.6.cloned.1.call-start
  12.3 0.7 all-gather.6.cloned.1.call-update
  13.0 0.0 reduce-scatter.2.cloned.1.call-start
  13.1 0.6 dynamic-slice
  14.4 0.2 dynamic-update-slice
  14.6 132.0 %all-reduce = f32[512]{0:T(512)S(1)} all-reduce(f32[512]{0:T(512)S(1)} %dynamic-update-slice), channel_id=2, replica_groups=mesh['seq'=64,'pool'=4] {'seq'}, use_global_device_ids=true, to_apply=%add | all-reduce | flops 512 | bytes 4096
  146.6 0.1 reshape.211
  146.7 1.3 copy.51
  148.0 0.1 iota_compare_fusion
  148.1 10.6 %all-gather.10.cloned.1.call-done = f32[512,128,128]{2,1,0:T(8,128)} async-done(((f32[8,128,128]{2,1,0:T(8,128)}), f32[512,128,128]{2,1,0:T(8,128)}) %all-gather.10.cloned.1.call-update) | async-done | bytes 33554448 | tf_op jit(solution)/shard_map/all_gather | solution.py:13
  158.8 1.2 while.12
  158.8 1.2 bitcast_add_fusion.3
  160.0 2.4 fusion.11
  162.4 7.4 %fusion.5 = (f32[8,512]{1,0:T(8,128)S(1)}, f32[8,512,128]{1,2,0:T(8,128)}) fusion(f32[8,128,512]{2,1,0:T(8,128)} %fusion.11, f32[8,512]{1,0:T(8,128)S(1)} %get-tuple-element.62, bf16[8,512,128]{2,0,1:T(8,128)(2,1)} %bitcast.94, f32[8,512]{1,0:T(8,128)S(1)} %get-tuple-element.61, pred[512,512]{1,0:T(8,128)(4,1)S(1)} %iota_compare_fusion, ...), kind=kOutput, calls=%fused_computation.8 | convolution fusion | flops 1086320640 | bytes 7651328 | tf_op jit(solution)/shard_map/hij,hjd->hid/dot_general | solution.py:53
  169.9 2.2 fusion.8
  172.1 69.3 %all-gather.6.cloned.1.call-done = bf16[1024,4096]{0,1:T(8,128)(2,1)} async-done(((bf16[1024,64]{0,1:T(8,128)(2,1)}), bf16[1024,4096]{0,1:T(8,128)(2,1)}) %all-gather.6.cloned.1.call-update) | async-done | bytes 8388624 | tf_op jit(solution)/shard_map/all_gather | solution.py:91
  241.4 10.3 %fusion.25 = f32[512,4096]{1,0:T(8,128)} fusion(bf16[512,1024]{0,1:T(8,128)(2,1)S(1)} %bitcast.90, bf16[1024,4096]{0,1:T(8,128)(2,1)} %all-gather.6.cloned.1.call-done), kind=kOutput, calls=%fused_computation.50 | convolution fusion | flops 4294967296 | bytes 17825792 | tf_op jit(solution)/shard_map/dot_general | solution.py:89
  251.7 0.0 reduce-scatter.2.cloned.1.call-update
  251.7 0.0 copy-start.7
  251.7 0.0 all-gather.8.cloned.1.call-start
  251.8 0.5 all-gather.8.cloned.1.call-update
  252.3 0.0 copy-done.8
  252.4 0.6 fusion.24
  252.9 0.7 iota_compare_fusion.2
  253.6 0.7 iota_compare_fusion.1
  254.3 0.7 and_convert_fusion
  254.9 4.0 all-to-all-start
  258.9 78.1 %reduce-scatter.2.cloned.1.call-done = f32[128,4096]{1,0:T(8,128)} async-done(((f32[512,4096]{1,0:T(8,128)}), f32[128,4096]{1,0:T(8,128)}) %reduce-scatter.2.cloned.1.call-update) | async-done | bytes 2097168 | tf_op jit(solution)/shard_map/reduce_scatter | solution.py:94
  337.0 2.1 multiply_reduce_fusion
  339.1 83.8 %all-gather.8.cloned.1.call-done = bf16[4096,1024]{1,0:T(8,128)(2,1)} async-done(((bf16[64,1024]{1,0:T(8,128)(2,1)}), bf16[4096,1024]{1,0:T(8,128)(2,1)}) %all-gather.8.cloned.1.call-update) | async-done | bytes 8388624 | tf_op jit(solution)/shard_map/all_gather | solution.py:110
  422.9 4.7 %convolution_convert_fusion.1 = bf16[128,1024]{1,0:T(8,128)(2,1)S(1)} fusion(bf16[4096,1024]{1,0:T(8,128)(2,1)} %all-gather.8.cloned.1.call-done, f32[128,4096]{1,0:T(8,128)S(1)} %copy-done.2, bf16[128,4096]{1,0:T(8,128)(2,1)S(1)} %copy-done.3, f32[4096]{0:T(1024)S(1)} %copy-done.7, f32[128]{0:T(128)S(1)} %add_rsqrt_fusion), kind=kOutput, calls=%fused_computation.20 | convolution fusion | flops 1076494336 | bytes 11813376 | tf_op jit(solution)/shard_map/dot_general | solution.py:108
  427.6 0.0 copy-start.1
  427.6 1.1 broadcast_select_fusion
  428.8 0.0 all-to-all-done
  428.8 4.0 all-to-all-start.1
  432.7 0.1 copy.34
  432.8 14.5 %all-to-all-done.1 = bf16[4,1,128,1024]{3,2,1,0:T(8,128)(2,1)S(1)} async-done(((bf16[4,1,128,1024]{3,2,1,0:T(8,128)(2,1)}), bf16[4,1,128,1024]{3,2,1,0:T(8,128)(2,1)S(1)}, u32[]{:S(2)}, u32[]{:S(2)}) %all-to-all-start.1) | async-done | bytes 1048608 | tf_op jit(solution)/shard_map/all_to_all | solution.py:119
  447.4 0.9 fusion.9
  448.3 0.9 copy.42
  (25 shorter events, 0.1 us)
Async XLA Ops:
  6.5 153.5 %copy-start = (bf16[512,1024]{1,0:T(8,128)(2,1)S(1)}, bf16[512,1024]{1,0:T(8,128)(2,1)}, u32[]{:S(2)}) copy-start(bf16[512,1024]{1,0:T(8,128)(2,1)} %param.11) | copy-start | bytes 3145732
  6.5 4.4 copy-start.5
  6.5 152.2 %all-gather.10.cloned.1.call-start = ((), (), s32[]{:S(2)}) async-start(), calls=%async_computation.6 | async-start | bytes 34078720 | tf_op jit(solution)/shard_map/all_gather | solution.py:13
  11.0 137.1 %copy-start.6 = (bf16[512,1024]{0,1:T(8,128)(2,1)}, bf16[512,1024]{0,1:T(8,128)(2,1)S(1)}, u32[]{:S(2)}) copy-start(bf16[512,1024]{0,1:T(8,128)(2,1)S(1)} %copy.46) | copy-start | bytes 3145732
  11.0 2.1 copy-start.9
  12.3 229.1 %all-gather.6.cloned.1.call-start = ((), (), s32[]{:S(2)}) async-start(), calls=%async_computation.3 | async-start | bytes 8519680 | tf_op jit(solution)/shard_map/all_gather | solution.py:91
  13.0 324.0 %reduce-scatter.2.cloned.1.call-start = ((), (), s32[]{:S(2)}) async-start(), calls=%async_computation.4 | async-start | bytes 10485760 | tf_op jit(solution)/shard_map/reduce_scatter | solution.py:94
  162.4 7.5 %copy-start.4 = (f32[8,128,512]{2,1,0:T(8,128)S(1)}, f32[8,128,512]{2,1,0:T(8,128)}, u32[]{:S(2)}) copy-start(f32[8,128,512]{2,1,0:T(8,128)} %fusion.11) | copy-start | bytes 6291460
  251.7 0.7 copy-start.8
  251.7 85.3 %copy-start.3 = (bf16[128,4096]{1,0:T(8,128)(2,1)S(1)}, bf16[128,4096]{1,0:T(8,128)(2,1)}, u32[]{:S(2)}) copy-start(bf16[128,4096]{1,0:T(8,128)(2,1)} %param.15) | copy-start | bytes 3145732
  251.7 171.2 %copy-start.7 = (f32[4096]{0:T(1024)S(1)}, f32[4096]{0:T(1024)}, u32[]{:S(2)}) copy-start(f32[4096]{0:T(1024)} %param.17) | copy-start | bytes 49156
  251.7 171.2 %all-gather.8.cloned.1.call-start = ((), (), s32[]{:S(2)}) async-start(), calls=%async_computation.5 | async-start | bytes 8519680 | tf_op jit(solution)/shard_map/all_gather | solution.py:110
  254.9 173.8 %all-to-all-start = ((bf16[4,1,2]{2,1,0:T(2,128)(2,1)}), bf16[4,1,2]{2,1,0:T(2,128)(2,1)S(1)}, u32[]{:S(2)}, u32[]{:S(2)}) async-start(bf16[4,1,2]{2,1,0:T(2,128)(2,1)} %and_convert_fusion), calls=%async_computation | async-start | bytes 4096 | tf_op jit(solution)/shard_map/all_to_all | solution.py:120
  337.0 85.9 %copy-start.2 = (f32[128,4096]{1,0:T(8,128)S(1)}, f32[128,4096]{1,0:T(8,128)}, u32[]{:S(2)}) copy-start(f32[128,4096]{1,0:T(8,128)} %reduce-scatter.2.cloned.1.call-done) | copy-start | bytes 6291460
  427.6 21.6 %copy-start.1 = (bf16[512,1024]{1,0:T(8,128)(2,1)S(1)}, bf16[512,1024]{1,0:T(8,128)(2,1)}, u32[]{:S(2)}) copy-start(bf16[512,1024]{1,0:T(8,128)(2,1)} %param.11) | copy-start | bytes 3145732
  428.8 18.6 %all-to-all-start.1 = ((bf16[4,1,128,1024]{3,2,1,0:T(8,128)(2,1)}), bf16[4,1,128,1024]{3,2,1,0:T(8,128)(2,1)S(1)}, u32[]{:S(2)}, u32[]{:S(2)}) async-start(bf16[4,1,128,1024]{3,2,1,0:T(8,128)(2,1)} %broadcast_select_fusion), calls=%async_computation.2 | async-start | bytes 2097152 | tf_op jit(solution)/shard_map/all_to_all | solution.py:119
Sparse Core Ops, SparseCore 0:
  12.4 146.2 all-gather.9
  161.5 79.8 all-gather.5
  251.9 85.1 reduce-scatter.1
  339.7 83.2 all-gather.7
where the time goes:
time: 459 us; the launch traced here: 456 us
  waiting for transfers between devices  258 us (56%)
  blocking collectives  132 us (29%)
  matrix products  27 us (6%)
  between operations  13.9 us (3%)
  other arithmetic  11.2 us (2%)
  starting transfers between devices  8.06 us (2%)
  local copies, waits for them, and re-layouts  5.81 us (1%)
    unnamed x1, blocking collectives  132 us
    all_gather x1, waiting for transfers between devices, on_device(): lax.all_gather(kv_weight, 'seq', axis=0, tiled=True)  83.8 us
    reduce_scatter x1, waiting for transfers between devices, on_device(): lax.psum_scatter(partial_value, 'pool', scatter_dimension=0, tiled=True)  78.1 us
    all_gather x1, waiting for transfers between devices, on_device(): lax.all_gather(out_weight, 'seq', axis=1, tiled=True)  69.3 us
    all_to_all x1, waiting for transfers between devices, on_device(): lax.all_to_all(outgoing, 'pool', split_axis=0, concat_axis=0, tiled=True)  14.5 us
    all_gather x1, waiting for transfers between devices, entering(): gathered = jax.tree.map(lambda a: lax.all_gather(a, axis), part)  10.6 us
    dot_general x1, matrix products, on_device(): jnp.dot(mixed_list, lax.all_gather(out_weight, 'seq', axis=1, tiled=True)...  10.3 us
  transfers between devices with their start and end apart: 6, of which 5 were waited for; matrix products, arithmetic and copies ran while one was open for 6% of the time, Pallas kernels for 0%

commit v1 on v0

--- a/solution.py
+++ b/solution.py
@@ -88,7 +88,9 @@
     mixed_list = scaled.transpose(1, 0, 2).reshape(BLK, head_count * HD).astype(jnp.bfloat16)
     partial_value = jnp.dot(
         mixed_list,
-        lax.all_gather(out_weight, "seq", axis=1, tiled=True),
+        jnp.concatenate(
+            lax.all_to_all(jnp.stack([out_weight] * lax.axis_size("seq")), "seq", 0, 0), axis=1
+        ),
         preferred_element_type=jnp.float32,
     )
     summed = lax.psum_scatter(partial_value, "pool", scatter_dimension=0, tiled=True)

time: 459 us -> 706 us (1.54)
  blocking collectives: 132 us -> 371 us
  starting transfers between devices: 8.06 us -> 21.7 us
  waiting for transfers between devices: 258 us -> 248 us
    unnamed x1, blocking collectives: 132 us -> 371 us
    reduce_scatter x1, waiting for transfers between devices: 78.1 us -> 148 us  [on_device(): lax.psum_scatter(partial_value, 'pool', scatter_dimension=0, tiled=True)]
    all_gather x1 -> x0, waiting for transfers between devices: 69.3 us -> none  [on_device(): lax.all_gather(out_weight, 'seq', axis=1, tiled=True)]
    all_to_all x0 -> x1, starting transfers between devices: none -> 13.5 us  [on_device(): lax.all_to_all(jnp.stack([out_weight] * lax.axis_size('seq')), 'seq', 0, 0)]
    all_gather x1, waiting for transfers between devices: 10.6 us -> 0.02 us  [entering(): gathered = jax.tree.map(lambda a: lax.all_gather(a, axis), part)]
  transfers between devices with their start and end apart: 6 -> 6, of which waited for: 5 -> 3; matrix products, arithmetic and copies ran while one was open for 6% -> 4% of each run, Pallas kernels for 0% -> 0%
where the time goes in v1:
time: 706 us; the launch traced here: 702 us
  blocking collectives  371 us (53%)
  waiting for transfers between devices  248 us (35%)
  matrix products  27 us (4%)
  starting transfers between devices  21.7 us (3%)
  between operations  14 us (2%)
  other arithmetic  11.2 us (2%)
  local copies, waits for them, and re-layouts  10.1 us (1%)
    unnamed x1, blocking collectives  371 us
    reduce_scatter x1, waiting for transfers between devices, on_device(): lax.psum_scatter(partial_value, 'pool', scatter_dimension=0, tiled=True)  148 us
    all_gather x1, waiting for transfers between devices, on_device(): lax.all_gather(kv_weight, 'seq', axis=0, tiled=True)  84 us
    all_to_all x1, waiting for transfers between devices, on_device(): lax.all_to_all(outgoing, 'pool', split_axis=0, concat_axis=0, tiled=True)  14.5 us
  transfers between devices with their start and end apart: 6, of which 3 were waited for; matrix products, arithmetic and copies ran while one was open for 4% of the time, Pallas kernels for 0%

profile of v1, /device:TPU:1, one launch (start us, length us, event | category | flops | bytes accessed | tf_op | source)
XLA Modules:
  0.0 702.2 jit_solution(15287521809159446918)
XLA Ops:
  6.5 2.4 reduce-window.6
  8.9 0.2 slice_reduce_fusion
  9.1 0.1 exponential_bitcast_fusion.1
  9.2 0.2 slice_reduce_fusion.1
  9.4 0.1 fusion.23
  9.5 1.5 copy.47
  11.0 0.0 copy-start.7
  11.0 1.3 convolution_add_fusion
  12.3 0.0 all-gather.7.cloned.1.call-update
  12.3 4.3 stack.2
  16.6 13.5 %all-to-all-start.1 = ((bf16[64,1024,64]{1,2,0:T(8,128)(2,1)}), bf16[64,1024,64]{1,2,0:T(8,128)(2,1)}, u32[]{:S(2)}, u32[]{:S(2)}) async-start(bf16[64,1024,64]{1,2,0:T(8,128)(2,1)} %stack.2), calls=%async_computation.1 | async-start | bytes 16777216 | tf_op jit(solution)/shard_map/all_to_all | solution.py:92
  30.1 0.0 reduce-scatter.2.cloned.1.call-start
  30.1 0.6 dynamic-slice
  31.4 0.2 dynamic-update-slice
  31.6 370.7 %all-reduce = f32[512]{0:T(512)S(1)} all-reduce(f32[512]{0:T(512)S(1)} %dynamic-update-slice), channel_id=2, replica_groups=mesh['seq'=64,'pool'=4] {'seq'}, use_global_device_ids=true, to_apply=%add | all-reduce | flops 512 | bytes 4096
  402.3 0.1 reshape.221
  402.4 1.3 copy.52
  403.7 0.1 iota_compare_fusion
  403.8 0.0 all-gather.7.cloned.1.call-done
  403.8 1.2 while.12
  403.9 1.2 bitcast_add_fusion.3
  405.1 2.4 fusion.11
  407.5 7.4 %fusion.5 = (f32[8,512]{1,0:T(8,128)S(1)}, f32[8,512,128]{1,2,0:T(8,128)}) fusion(f32[8,128,512]{2,1,0:T(8,128)} %fusion.11, f32[8,512]{1,0:T(8,128)S(1)} %get-tuple-element.62, bf16[8,512,128]{2,0,1:T(8,128)(2,1)} %bitcast.97, f32[8,512]{1,0:T(8,128)S(1)} %get-tuple-element.61, pred[512,512]{1,0:T(8,128)(4,1)S(1)} %iota_compare_fusion, ...), kind=kOutput, calls=%fused_computation.8 | convolution fusion | flops 1086320640 | bytes 7651328 | tf_op jit(solution)/shard_map/hij,hjd->hid/dot_general | solution.py:53
  414.9 0.0 copy-done.4
  415.0 2.2 fusion.8
  417.1 0.0 all-to-all-done.1
  417.1 10.3 %fusion.25 = f32[512,4096]{1,0:T(8,128)} fusion(bf16[512,1024]{0,1:T(8,128)(2,1)S(1)} %bitcast.93, bf16[1024,4096]{0,1:T(8,128)(2,1)} %bitcast.23), kind=kOutput, calls=%fused_computation.50 | convolution fusion | flops 4294967296 | bytes 17825792 | tf_op jit(solution)/shard_map/dot_general | solution.py:89
  427.4 0.0 reduce-scatter.2.cloned.1.call-update
  427.5 0.0 copy-start.8
  427.5 0.0 all-gather.5.cloned.1.call-start
  427.5 0.7 all-gather.5.cloned.1.call-update
  428.2 0.6 fusion.24
  428.8 0.7 iota_compare_fusion.2
  429.5 0.7 iota_compare_fusion.1
  430.2 0.7 and_convert_fusion
  430.8 4.2 all-to-all-start
  435.0 148.4 %reduce-scatter.2.cloned.1.call-done = f32[128,4096]{1,0:T(8,128)} async-done(((f32[512,4096]{1,0:T(8,128)}), f32[128,4096]{1,0:T(8,128)}) %reduce-scatter.2.cloned.1.call-update) | async-done | bytes 2097168 | tf_op jit(solution)/shard_map/reduce_scatter | solution.py:96
  583.4 2.1 multiply_reduce_fusion
  585.5 84.0 %all-gather.5.cloned.1.call-done = bf16[4096,1024]{1,0:T(8,128)(2,1)} async-done(((bf16[64,1024]{1,0:T(8,128)(2,1)}), bf16[4096,1024]{1,0:T(8,128)(2,1)}) %all-gather.5.cloned.1.call-update) | async-done | bytes 8388624 | tf_op jit(solution)/shard_map/all_gather | solution.py:112
  669.4 4.7 convolution_convert_fusion.1
  674.1 0.0 copy-start.1
  674.1 1.1 broadcast_select_fusion
  675.2 0.0 all-to-all-done
  675.2 4.0 all-to-all-start.2
  679.2 0.1 copy.35
  679.3 14.5 %all-to-all-done.2 = bf16[4,1,128,1024]{3,2,1,0:T(8,128)(2,1)S(1)} async-done(((bf16[4,1,128,1024]{3,2,1,0:T(8,128)(2,1)}), bf16[4,1,128,1024]{3,2,1,0:T(8,128)(2,1)S(1)}, u32[]{:S(2)}, u32[]{:S(2)}) %all-to-all-start.2) | async-done | bytes 1048608 | tf_op jit(solution)/shard_map/all_to_all | solution.py:121
  693.9 0.9 fusion.9
  694.8 0.9 copy.43
  (27 shorter events, 0.2 us)
Async XLA Ops:
  6.5 398.6 %copy-start = (bf16[512,1024]{1,0:T(8,128)(2,1)S(1)}, bf16[512,1024]{1,0:T(8,128)(2,1)}, u32[]{:S(2)}) copy-start(bf16[512,1024]{1,0:T(8,128)(2,1)} %param.11) | copy-start | bytes 3145732
  6.5 4.4 copy-start.5
  6.5 397.3 %all-gather.7.cloned.1.call-start = ((), (), s32[]{:S(2)}) async-start(), calls=%async_computation.6 | async-start | bytes 34078720 | tf_op jit(solution)/shard_map/all_gather | solution.py:13
  11.0 5.6 copy-start.6
  11.0 1.3 copy-start.7
  16.6 13.5 %copy-start.10 = (u32[256]{0:T(256)S(1)}, u32[256]{0:T(256)}, u32[]{:S(2)}) copy-start(u32[256]{0:T(256)} %constant.48) | copy-start | bytes 3076
  16.6 400.5 %all-to-all-start.1 = ((bf16[64,1024,64]{1,2,0:T(8,128)(2,1)}), bf16[64,1024,64]{1,2,0:T(8,128)(2,1)}, u32[]{:S(2)}, u32[]{:S(2)}) async-start(bf16[64,1024,64]{1,2,0:T(8,128)(2,1)} %stack.2), calls=%async_computation.1 | async-start | bytes 16777216 | tf_op jit(solution)/shard_map/all_to_all | solution.py:92
  30.1 553.3 %reduce-scatter.2.cloned.1.call-start = ((), (), s32[]{:S(2)}) async-start(), calls=%async_computation.4 | async-start | bytes 10485760 | tf_op jit(solution)/shard_map/reduce_scatter | solution.py:96
  407.5 7.5 %copy-start.4 = (f32[8,128,512]{2,1,0:T(8,128)S(1)}, f32[8,128,512]{2,1,0:T(8,128)}, u32[]{:S(2)}) copy-start(f32[8,128,512]{2,1,0:T(8,128)} %fusion.11) | copy-start | bytes 6291460
  427.4 0.8 copy-start.9
  427.4 155.9 %copy-start.3 = (bf16[128,4096]{1,0:T(8,128)(2,1)S(1)}, bf16[128,4096]{1,0:T(8,128)(2,1)}, u32[]{:S(2)}) copy-start(bf16[128,4096]{1,0:T(8,128)(2,1)} %param.15) | copy-start | bytes 3145732
  427.5 242.0 %copy-start.8 = (f32[4096]{0:T(1024)S(1)}, f32[4096]{0:T(1024)}, u32[]{:S(2)}) copy-start(f32[4096]{0:T(1024)} %param.17) | copy-start | bytes 49156
  427.5 241.9 %all-gather.5.cloned.1.call-start = ((), (), s32[]{:S(2)}) async-start(), calls=%async_computation.5 | async-start | bytes 8519680 | tf_op jit(solution)/shard_map/all_gather | solution.py:112
  430.8 244.4 %all-to-all-start = ((bf16[4,1,2]{2,1,0:T(2,128)(2,1)}), bf16[4,1,2]{2,1,0:T(2,128)(2,1)S(1)}, u32[]{:S(2)}, u32[]{:S(2)}) async-start(bf16[4,1,2]{2,1,0:T(2,128)(2,1)} %and_convert_fusion), calls=%async_computation | async-start | bytes 4096 | tf_op jit(solution)/shard_map/all_to_all | solution.py:122
  583.4 86.1 %copy-start.2 = (f32[128,4096]{1,0:T(8,128)S(1)}, f32[128,4096]{1,0:T(8,128)}, u32[]{:S(2)}) copy-start(f32[128,4096]{1,0:T(8,128)} %reduce-scatter.2.cloned.1.call-done) | copy-start | bytes 6291460
  674.1 21.6 %copy-start.1 = (bf16[512,1024]{1,0:T(8,128)(2,1)S(1)}, bf16[512,1024]{1,0:T(8,128)(2,1)}, u32[]{:S(2)}) copy-start(bf16[512,1024]{1,0:T(8,128)(2,1)} %param.11) | copy-start | bytes 3145732
  675.2 18.6 %all-to-all-start.2 = ((bf16[4,1,128,1024]{3,2,1,0:T(8,128)(2,1)}), bf16[4,1,128,1024]{3,2,1,0:T(8,128)(2,1)S(1)}, u32[]{:S(2)}, u32[]{:S(2)}) async-start(bf16[4,1,128,1024]{3,2,1,0:T(8,128)(2,1)} %broadcast_select_fusion), calls=%async_computation.3 | async-start | bytes 2097152 | tf_op jit(solution)/shard_map/all_to_all | solution.py:121
Sparse Core Ops, SparseCore 0:
  12.4 302.3 all-gather.6
  427.6 155.7 reduce-scatter.1
  586.1 83.2 all-gather.4
